TPU v7x, 768 devices: a whole 4x8x12 slice. The times are simulated.
768 devices in a mesh: ctx: 16 (over y, core), chan: 48 (over x, z).
Axes of the slice: x: 4, y: 8, z: 12, core: 2. Of those that a mesh axis runs over, the one named last changes fastest.
Arguments:
- queries: bfloat16 [1, 32768, 6144], P(None, 'ctx', 'chan')
- keys_in: bfloat16 [1, 32768, 6144], P(None, 'ctx', 'chan'), may hold values from -6 to 6
- values_in: bfloat16 [1, 32768, 6144], P(None, 'ctx', 'chan'), may hold values from -6 to 6
- short_weights: float32 [3, 7, 6144], P(None, None, 'chan'), may hold values from -2 to 2
- decay_rates: float32 [16, 6144], P(None, 'chan'), may hold values from 1.4953613e-06 to 0.0334, as said below
- residues: float32 [16, 6144], P(None, 'chan'), may hold values from -1.5 to 1.5
- skip_term: float32 [6144], P('chan'), may hold values from -1 to 1
- out_gain: float32 [6144], P('chan'), may hold values from 0.25 to 1.75
Outputs:
- normed: bfloat16 [1, 32768, 6144], P(None, 'ctx', 'chan')
Inputs may be any that keep to these rules, and one draw needn't show every extreme that they name: `decay_rates`: each rate is positive.
All inputs are finite; a program needn't handle non-finite values.
Results may differ from a plain program's by a relative error of at most 0.0065.
Values may be sent and summed in bfloat16 or wider, within the bound.
A program may use at most 32 MiB of HBM per device.

v0:
```python
import functools

import jax
import jax.numpy as jnp
from jax import lax
from jax.experimental import pallas as pl
from jax.experimental.pallas import tpu as pltpu
from jax.sharding import PartitionSpec as P

MESH = pl.DeviceIdType.MESH
F32 = jnp.float32
BF16 = jnp.bfloat16
SEG = 8
LANES = 128
UNROLL = 8
HALO = 16
X_CHIPS = 4


def expm1_of_minus(x):
    series = jnp.full_like(x, 1.0 / 40320.0)
    for factor in (5040.0, 720.0, 120.0, 24.0, 6.0, 2.0, 1.0):
        series = 1.0 / factor - x * series
    return jnp.where(x < 0.25, x * series, 1.0 - jnp.exp(-x))


def per_mode(rows):
    return jnp.broadcast_to(rows[:, None, :], (rows.shape[0], SEG, rows.shape[1]))


def body(
    sizes,
    q_hbm,
    k_hbm,
    v_hbm,
    w_hbm,
    lam_hbm,
    res_hbm,
    skip_hbm,
    gain_hbm,
    out_hbm,
    raw,
    nat,
    w_ref,
    lam_ref,
    res_ref,
    skip_ref,
    gain_ref,
    halo,
    u_ref,
    qs_ref,
    y_ref,
    mix_ref,
    pow_ref,
    send_state,
    got_state,
    send_x,
    got_x,
    send_z,
    got_z,
    out_v,
    in_sem,
    par_sem,
    halo_s,
    halo_r,
    st_s,
    st_r,
    x_s,
    x_r,
    z_s,
    z_r,
    out_sem,
):
    n_ctx, n_chan, width, taps, modes = sizes
    rows = q_hbm.shape[0]
    steps = rows // SEG
    z_chips = n_chan // X_CHIPS
    ctx = lax.axis_index("ctx")
    chan = lax.axis_index("chan")
    my_x, my_z = chan // z_chips, chan % z_chips

    def along_ctx(k):
        return ((ctx + k) % n_ctx, chan)

    def along_x(k):
        return (ctx, ((my_x + k) % X_CHIPS) * z_chips + my_z)

    def along_z(k):
        return (ctx, my_x * z_chips + (my_z + k) % z_chips)

    barrier = pltpu.get_barrier_semaphore()
    for k in range(1, n_ctx):
        pl.semaphore_signal(barrier, inc=1, device_id=along_ctx(k), device_id_type=MESH)
    for k in range(1, X_CHIPS):
        pl.semaphore_signal(barrier, inc=1, device_id=along_x(k), device_id_type=MESH)
    for k in range(1, z_chips):
        pl.semaphore_signal(barrier, inc=1, device_id=along_z(k), device_id_type=MESH)

    streams = (q_hbm, k_hbm, v_hbm)
    params = [
        pltpu.make_async_copy(src, dst, par_sem.at[i])
        for i, (src, dst) in enumerate(
            (
                (w_hbm, w_ref),
                (lam_hbm, lam_ref),
                (res_hbm, res_ref),
                (skip_hbm, skip_ref),
                (gain_hbm, gain_ref),
            )
        )
    ]
    loads = [pltpu.make_async_copy(streams[i], raw.at[i], in_sem.at[i]) for i in range(3)]
    loads[1].start()
    loads[2].start()
    for copy in params:
        copy.start()
    loads[0].start()
    for copy in params:
        copy.wait()

    lam = lam_ref[...]
    coef = res_ref[...] * jnp.sqrt(expm1_of_minus(2.0 * lam))
    decay = 1.0 - expm1_of_minus(lam)

    def to_natural(i):
        def convert(r, carry):
            start = pl.multiple_of(r * 64, 64)
            nat[i, pl.ds(8 + start, 64), :] = raw[i, pl.ds(start, 64), :].astype(F32)
            return carry

        lax.fori_loop(0, rows // 64, convert, 0)

    def tap(i, j):
        return jnp.broadcast_to(w_ref[i, j : j + 1, :], (SEG, width))

    def filtered(i, weights, t0):
        window = [
            nat[i, pl.ds(t0 + 2 + k + 7 - taps, SEG, stride=steps), :]
            for k in range(UNROLL + taps - 1)
        ]
        results = []
        for t in range(UNROLL):
            total = weights[0] * window[t + taps - 1]
            for j in range(1, taps):
                total = total + weights[j] * window[t + taps - 1 - j]
            results.append(total)
        return results

    loads[1].wait()
    to_natural(1)
    loads[2].wait()
    to_natural(2)

    w_k = [tap(1, j) for j in range(taps)]
    w_v = [tap(2, j) for j in range(taps)]

    def make_u(t0):
        ks = filtered(1, w_k, t0)
        vs = filtered(2, w_v, t0)
        for t in range(UNROLL):
            u_ref[t0 + t] = ks[t] * vs[t]

    def u_chunk(c, carry):
        make_u(pl.multiple_of(c * UNROLL, UNROLL))
        return carry

    lax.fori_loop(1, steps // UNROLL, u_chunk, 0)

    decay_b = per_mode(decay)

    def advance(t0, state):
        for t in range(UNROLL):
            state = decay_b * state + u_ref[t0 + t][None]
        return state

    def end_chunk(c, state):
        return advance(pl.multiple_of(c * UNROLL, UNROLL), state)

    zero_state = jnp.zeros((modes, SEG, width), F32)
    ends = lax.fori_loop(1, steps // UNROLL, end_chunk, zero_state)

    pl.semaphore_wait(barrier, (n_ctx - 1) + (X_CHIPS - 1) + (z_chips - 1))
    halos = [
        pltpu.make_async_remote_copy(
            src_ref=streams[i].at[pl.ds(rows - HALO, HALO)],
            dst_ref=halo.at[i],
            send_sem=halo_s.at[i],
            recv_sem=halo_r.at[i],
            device_id=along_ctx(1),
            device_id_type=MESH,
        )
        for i in range(3)
    ]
    for copy in halos:
        copy.start()
    loads[0].wait()
    to_natural(0)
    for copy in halos:
        copy.wait()
    has_before = (ctx > 0).astype(F32)
    for i in range(3):
        nat[i, 0:8, :] = halo[i].astype(F32)[8:16] * has_before

    make_u(0)
    first = advance(0, zero_state)
    ends = ends + per_mode(jnp.exp(lam * (-1.0 * (steps - UNROLL)))) * first

    segment = lax.broadcasted_iota(jnp.int32, (modes, SEG, width), 1)
    total = ends
    for shift in (1, 2, 4):
        weight = jnp.where(
            segment >= shift, per_mode(jnp.exp(lam * (-1.0 * steps * shift))), 0.0
        )
        total = total + weight * pltpu.roll(total, shift, 1)
    send_state[...] = total[:, SEG - 1, :].astype(BF16)
    start = jnp.where(segment >= 1, pltpu.roll(total, 1, 1), 0.0)

    states = [
        pltpu.make_async_remote_copy(
            src_ref=send_state,
            dst_ref=got_state.at[k],
            send_sem=st_s.at[k],
            recv_sem=st_r.at[k],
            device_id=along_ctx(k),
            device_id_type=MESH,
        )
        for k in range(1, n_ctx)
    ]
    for k in sorted(range(1, n_ctx), key=lambda k: abs(k - n_ctx // 2)):
        states[k - 1].start()

    w_q = [tap(0, j) for j in range(taps)]

    def q_chunk(c, carry):
        t0 = pl.multiple_of(c * UNROLL, UNROLL)
        qs = filtered(0, w_q, t0)
        for t in range(UNROLL):
            qs_ref[t0 + t] = qs[t]
        return carry

    lax.fori_loop(0, steps // UNROLL, q_chunk, 0)

    coef_b = per_mode(coef)
    skip_b = jnp.broadcast_to(skip_ref[...], (SEG, width))

    def y_chunk(c, state):
        t0 = pl.multiple_of(c * UNROLL, UNROLL)
        for t in range(UNROLL):
            u = u_ref[t0 + t]
            state = decay_b * state + u[None]
            y_ref[t0 + t] = jnp.sum(coef_b * state, axis=0) + skip_b * u
        return state

    lax.fori_loop(0, steps // UNROLL, y_chunk, start)

    device_decay = jnp.exp(lam * (-1.0 * rows))
    lead = per_mode(coef) * jnp.exp(
        per_mode(lam) * (-1.0 * steps * segment.astype(F32))
    )
    for copy in states:
        copy.wait()
    incoming = jnp.zeros((modes, width), F32)
    for k in range(n_ctx - 1, 0, -1):
        reached = (ctx >= k).astype(F32)
        incoming = device_decay * incoming + got_state[k].astype(F32) * reached

    def mix_chunk(c, far):
        t0 = pl.multiple_of(c * UNROLL, UNROLL)
        for t in range(UNROLL):
            far = decay_b * far
            mixed = qs_ref[t0 + t] * (y_ref[t0 + t] + jnp.sum(far, axis=0))
            mix_ref[pl.ds(t0 + t, SEG, stride=steps), :] = mixed
        return far

    lax.fori_loop(0, steps // UNROLL, mix_chunk, lead * per_mode(incoming))

    groups = rows // LANES
    ones = jnp.ones((2 * width, width), BF16)
    eye = (
        lax.broadcasted_iota(jnp.int32, (LANES, LANES), 0)
        == lax.broadcasted_iota(jnp.int32, (LANES, LANES), 1)
    )

    def power_group(g, carry):
        mixed = mix_ref[pl.ds(pl.multiple_of(g * LANES, LANES), LANES), :]
        square = mixed * mixed
        high = square.astype(BF16)
        low = (square - high.astype(F32)).astype(BF16)
        summed = jnp.dot(
            jnp.concatenate([high, low], axis=1), ones, preferred_element_type=F32
        )
        pow_ref[pl.ds(g, 1), :] = jnp.sum(jnp.where(eye, summed, 0.0), axis=0, keepdims=True)
        return carry

    lax.fori_loop(0, groups, power_group, 0)

    own = pow_ref[...]
    send_x[...] = own
    over_x = [
        pltpu.make_async_remote_copy(
            src_ref=send_x,
            dst_ref=got_x.at[k],
            send_sem=x_s.at[k],
            recv_sem=x_r.at[k],
            device_id=along_x(k),
            device_id_type=MESH,
        )
        for k in range(1, X_CHIPS)
    ]
    for copy in over_x:
        copy.start()
    for copy in over_x:
        copy.wait()
    own = own + sum(got_x[k] for k in range(1, X_CHIPS))
    send_z[...] = own.astype(BF16)
    over_z = [
        pltpu.make_async_remote_copy(
            src_ref=send_z,
            dst_ref=got_z.at[k],
            send_sem=z_s.at[k],
            recv_sem=z_r.at[k],
            device_id=along_z(k),
            device_id_type=MESH,
        )
        for k in range(1, z_chips)
    ]
    for k in sorted(range(1, z_chips), key=lambda k: abs(k - z_chips // 2)):
        over_z[k - 1].start()
    for copy in over_z:
        copy.wait()
    everything = own + sum(got_z[k].astype(F32) for k in range(1, z_chips))
    scale = lax.rsqrt(everything * (1.0 / (width * n_chan)) + 1e-05)

    padded = jnp.concatenate(
        [scale, jnp.zeros((LANES - groups, LANES), F32)], axis=0
    )
    columns = padded.T
    high = columns.astype(BF16)
    rest = columns - high.astype(F32)
    middle = rest.astype(BF16)
    low = (rest - middle.astype(F32)).astype(BF16)
    parts = jnp.concatenate([high, middle, low], axis=1)
    gain = gain_ref[...]
    part_row = lax.broadcasted_iota(jnp.int32, (3 * LANES, LANES), 0) % LANES

    outs = []
    for g in range(groups):
        pick = jnp.where(part_row == g, 1.0, 0.0).astype(BF16)
        spread = jnp.dot(parts, pick, preferred_element_type=F32)
        at = pl.ds(g * LANES, LANES)
        out_v[at, :] = (mix_ref[at, :] * spread * gain).astype(BF16)
        if g % 4 == 3:
            span = pl.ds((g - 3) * LANES, 4 * LANES)
            copy = pltpu.make_async_copy(out_v.at[span], out_hbm.at[span], out_sem.at[g // 4])
            copy.start()
            outs.append(copy)
    for copy in outs:
        copy.wait()


def shards(n_ctx, n_chan, queries, keys_in, values_in, short_weights, decay_rates, residues, skip_term, out_gain):
    rows, width = queries.shape[1:]
    taps, modes = short_weights.shape[1], decay_rates.shape[0]
    steps, groups = rows // SEG, rows // LANES
    z_chips = n_chan // X_CHIPS
    dma = pltpu.SemaphoreType.DMA
    out = pl.pallas_call(
        functools.partial(body, (n_ctx, n_chan, width, taps, modes)),
        out_shape=jax.ShapeDtypeStruct((rows, width), BF16),
        in_specs=[pl.BlockSpec(memory_space=pl.ANY)] * 8,
        out_specs=pl.BlockSpec(memory_space=pl.ANY),
        scratch_shapes=[
            pltpu.VMEM((3, rows, width), BF16),
            pltpu.VMEM((3, rows + 8, width), F32),
            pltpu.VMEM((3, taps, width), F32),
            pltpu.VMEM((modes, width), F32),
            pltpu.VMEM((modes, width), F32),
            pltpu.VMEM((1, width), F32),
            pltpu.VMEM((1, width), F32),
            pltpu.VMEM((3, HALO, width), BF16),
            pltpu.VMEM((steps, SEG, width), F32),
            pltpu.VMEM((steps, SEG, width), F32),
            pltpu.VMEM((steps, SEG, width), F32),
            pltpu.VMEM((rows, width), F32),
            pltpu.VMEM((groups, LANES), F32),
            pltpu.VMEM((modes, width), BF16),
            pltpu.VMEM((n_ctx, modes, width), BF16),
            pltpu.VMEM((groups, LANES), F32),
            pltpu.VMEM((X_CHIPS, groups, LANES), F32),
            pltpu.VMEM((groups, LANES), BF16),
            pltpu.VMEM((z_chips, groups, LANES), BF16),
            pltpu.VMEM((rows, width), BF16),
            dma((3,)),
            dma((5,)),
            dma((3,)),
            dma((3,)),
            dma((n_ctx,)),
            dma((n_ctx,)),
            dma((X_CHIPS,)),
            dma((X_CHIPS,)),
            dma((z_chips,)),
            dma((z_chips,)),
            dma((groups // 4,)),
        ],
        compiler_params=pltpu.CompilerParams(collective_id=0, has_side_effects=True),
        name="hyena",
    )(
        queries[0],
        keys_in[0],
        values_in[0],
        short_weights,
        decay_rates,
        residues,
        skip_term[None],
        out_gain[None],
    )
    return out[None]


def solution(mesh):
    placed = (
        P(None, "ctx", "chan"),
        P(None, "ctx", "chan"),
        P(None, "ctx", "chan"),
        P(None, None, "chan"),
        P(None, "chan"),
        P(None, "chan"),
        P("chan"),
        P("chan"),
    )
    return jax.shard_map(
        functools.partial(shards, mesh.shape["ctx"], mesh.shape["chan"]),
        mesh=mesh,
        in_specs=placed,
        out_specs=P(None, "ctx", "chan"),
        check_vma=False,
    )
```

profile of v0, /device:TPU:8, one launch (start us, length us, event | category | flops | bytes accessed | tf_op | source)
XLA Modules:
  0.0 44.0 jit_solution(11893941576959556774)
XLA Ops:
  0.0 42.1 %hyena.1 = bf16[2048,128]{1,0:T(8,128)(2,1)} custom-call(bf16[2048,128]{1,0:T(8,128)(2,1)} %bitcast.7, bf16[2048,128]{1,0:T(8,128)(2,1)} %bitcast.8, bf16[2048,128]{1,0:T(8,128)(2,1)} %bitcast.9, f32[3,7,128]{2,1,0:T(8,128)} %w_hbm.1, f32[16,128]{1,0:T(8,128)} %lam_hbm.1, f32[16,128]{1,0:T(8,128)} %res_hbm.1, f32[1,128]{1,0:T(1,128)} %bitcast.10, ...), custom_call_target="tpu_custom_call" | custom-call | tf_op jit(solution)/shard_map/hyena/pallas_call | solution.py:367
  42.1 1.9 %copy.10 = bf16[1,2048,128]{2,1,0:T(8,128)(2,1)} copy(bf16[1,2048,128]{2,1,0:T(8,128)(2,1)} %bitcast.6) | data formatting | bytes 1048576
where the time goes:
time: 44.1 us; the launch traced here: 44 us
  Pallas kernels  42.1 us (95%)
  local copies, waits for them, and re-layouts  1.87 us (4%)
    pallas_call x1, Pallas kernels, shards(): pl.pallas_call(functools.partial(body, (n_ctx, n_chan, width, taps, modes...  42.1 us
    unnamed x1, local copies, waits for them, and re-layouts  1.87 us

commit v1 on v0

v1 whole, which is shorter than its diff:
```python
import functools

import jax
import jax.numpy as jnp
from jax import lax
from jax.experimental import pallas as pl
from jax.experimental.pallas import tpu as pltpu
from jax.sharding import PartitionSpec as P

MESH = pl.DeviceIdType.MESH
F32 = jnp.float32
BF16 = jnp.bfloat16
SEG = 8
LANES = 128
CHUNK = 16
KEPT = 4
HALO = 16
X_CHIPS = 4


def expm1_of_minus(x):
    series = jnp.full_like(x, 1.0 / 40320.0)
    for factor in (5040.0, 720.0, 120.0, 24.0, 6.0, 2.0, 1.0):
        series = 1.0 / factor - x * series
    return jnp.where(x < 0.25, x * series, 1.0 - jnp.exp(-x))


def per_mode(rows):
    return jnp.broadcast_to(rows[:, None, :], (rows.shape[0], SEG, rows.shape[1]))


def over_modes(terms):
    while terms.shape[0] > 1:
        half = terms.shape[0] // 2
        terms = terms[:half] + terms[half:]
    return terms[0]


def in_all(row):
    return jnp.broadcast_to(row, (SEG, row.shape[-1]))


def body(
    sizes,
    q_hbm,
    k_hbm,
    v_hbm,
    w_hbm,
    lam_hbm,
    res_hbm,
    skip_hbm,
    gain_hbm,
    mix_ref,
    sum_ref,
    raw,
    w_ref,
    lam_ref,
    res_ref,
    skip_ref,
    gain_ref,
    halo,
    u_ref,
    qs_ref,
    y_ref,
    kept,
    out_pow,
    send_state,
    got_state,
    send_x,
    got_x,
    send_z,
    got_z,
    in_sem,
    par_sem,
    halo_s,
    halo_r,
    st_s,
    st_r,
    x_s,
    x_r,
    z_s,
    z_r,
):
    n_ctx, n_chan, width, taps, modes = sizes
    rows = q_hbm.shape[0]
    steps = rows // SEG
    chunks = steps // CHUNK
    rim = taps - 1
    z_chips = n_chan // X_CHIPS
    ctx = lax.axis_index("ctx")
    chan = lax.axis_index("chan")
    my_x, my_z = chan // z_chips, chan % z_chips

    def along_ctx(k):
        return ((ctx + k) % n_ctx, chan)

    def along_x(k):
        return (ctx, ((my_x + k) % X_CHIPS) * z_chips + my_z)

    def along_z(k):
        return (ctx, my_x * z_chips + (my_z + k) % z_chips)

    barrier = pltpu.get_barrier_semaphore()
    for k in range(1, n_ctx):
        pl.semaphore_signal(barrier, inc=1, device_id=along_ctx(k), device_id_type=MESH)
    for k in range(1, X_CHIPS):
        pl.semaphore_signal(barrier, inc=1, device_id=along_x(k), device_id_type=MESH)
    for k in range(1, z_chips):
        pl.semaphore_signal(barrier, inc=1, device_id=along_z(k), device_id_type=MESH)

    streams = (q_hbm, k_hbm, v_hbm)
    params = [
        pltpu.make_async_copy(src, dst, par_sem.at[i])
        for i, (src, dst) in enumerate(
            (
                (w_hbm, w_ref),
                (lam_hbm, lam_ref),
                (res_hbm, res_ref),
                (skip_hbm, skip_ref),
                (gain_hbm, gain_ref),
            )
        )
    ]
    loads = [pltpu.make_async_copy(streams[i], raw.at[i], in_sem.at[i]) for i in range(3)]
    loads[1].start()
    loads[2].start()
    for copy in params:
        copy.start()
    loads[0].start()
    for copy in params:
        copy.wait()

    lam = lam_ref[...]
    coef = res_ref[...] * jnp.sqrt(expm1_of_minus(2.0 * lam))
    decay = 1.0 - expm1_of_minus(lam)
    decay_b = per_mode(decay)
    coef_b = per_mode(coef)

    def by_step(i, c):
        parts = [
            raw[i, pl.ds(pl.multiple_of(s * steps + c * CHUNK, CHUNK), CHUNK), :]
            for s in range(SEG)
        ]
        return jnp.swapaxes(jnp.stack(parts).astype(F32), 0, 1)

    def taps_of(i):
        return [in_all(w_ref[i, j : j + 1, :]) for j in range(taps)]

    def filtered(weights, window):
        total = weights[0][None] * window[rim:]
        for j in range(1, taps):
            total = total + weights[j][None] * window[rim - j : rim - j + CHUNK]
        return total

    def make_u(c, before_k, before_v):
        window_k = jnp.concatenate([before_k, by_step(1, c)], axis=0)
        window_v = jnp.concatenate([before_v, by_step(2, c)], axis=0)
        at = pl.ds(pl.multiple_of(c * CHUNK, CHUNK), CHUNK)
        u_ref[at] = filtered(w_k, window_k) * filtered(w_v, window_v)
        return window_k[CHUNK:], window_v[CHUNK:]

    def u_chunk(c, before):
        return make_u(c, *before)

    loads[1].wait()
    loads[2].wait()
    w_k, w_v = taps_of(1), taps_of(2)
    first_k, first_v = by_step(1, 0)[CHUNK - rim :], by_step(2, 0)[CHUNK - rim :]
    before = lax.fori_loop(1, chunks // 2, u_chunk, (first_k, first_v))

    pl.semaphore_wait(barrier, (n_ctx - 1) + (X_CHIPS - 1) + (z_chips - 1))
    halos = [
        pltpu.make_async_remote_copy(
            src_ref=streams[i].at[pl.ds(rows - HALO, HALO)],
            dst_ref=halo.at[i],
            send_sem=halo_s.at[i],
            recv_sem=halo_r.at[i],
            device_id=along_ctx(1),
            device_id_type=MESH,
        )
        for i in range(3)
    ]
    for copy in halos:
        copy.start()
    tail_k, tail_v = lax.fori_loop(chunks // 2, chunks, u_chunk, before)

    def advance(c, state):
        for t in range(CHUNK):
            at = c * CHUNK + t
            if t % KEPT == 0:
                kept[c * (CHUNK // KEPT) + t // KEPT] = state
            state = decay_b * state + u_ref[at][None]
        return state

    zero_state = jnp.zeros((modes, SEG, width), F32)
    ends = lax.fori_loop(1, chunks, advance, zero_state)

    for copy in halos:
        copy.wait()
    has_before = (ctx > 0).astype(F32)
    top = lax.broadcasted_iota(jnp.int32, (rim, SEG, width), 1) == 0

    def entering(i, tail):
        rows_before = halo[i].astype(F32)[HALO - rim :] * has_before
        spread = jnp.broadcast_to(rows_before[:, None, :], (rim, SEG, width))
        return jnp.where(top, spread, pltpu.roll(tail, 1, 1))

    make_u(0, entering(1, tail_k), entering(2, tail_v))
    first = advance(0, zero_state)
    ends = ends + per_mode(jnp.exp(lam * (-1.0 * (steps - CHUNK)))) * first

    segment = lax.broadcasted_iota(jnp.int32, (modes, SEG, width), 1)
    total = ends
    for shift in (1, 2, 4):
        weight = jnp.where(
            segment >= shift, per_mode(jnp.exp(lam * (-1.0 * steps * shift))), 0.0
        )
        total = total + weight * pltpu.roll(total, shift, 1)
    send_state[...] = total[:, SEG - 1, :].astype(BF16)
    start = jnp.where(segment >= 1, pltpu.roll(total, 1, 1), 0.0)

    states = [
        pltpu.make_async_remote_copy(
            src_ref=send_state,
            dst_ref=got_state.at[k],
            send_sem=st_s.at[k],
            recv_sem=st_r.at[k],
            device_id=along_ctx(k),
            device_id_type=MESH,
        )
        for k in range(1, n_ctx)
    ]
    for k in sorted(range(1, n_ctx), key=lambda k: abs(k - n_ctx // 2)):
        states[k - 1].start()

    loads[0].wait()
    w_q = taps_of(0)

    def q_chunk(c, before_q):
        window = jnp.concatenate([before_q, by_step(0, c)], axis=0)
        at = pl.ds(pl.multiple_of(c * CHUNK, CHUNK), CHUNK)
        qs_ref[at] = filtered(w_q, window)
        return window[CHUNK:]

    tail_q = by_step(0, chunks - 1)[CHUNK - rim :]
    lax.fori_loop(0, chunks, q_chunk, entering(0, tail_q))

    response = []
    power_of = coef
    for i in range(KEPT):
        response.append(in_all(jnp.sum(power_of, axis=0, keepdims=True)))
        power_of = power_of * decay
        out_pow[i] = per_mode(power_of)
    response[0] = response[0] + in_all(skip_ref[...])

    def y_chunk(c, carry):
        for b in range(CHUNK // KEPT):
            state = kept[c * (CHUNK // KEPT) + b]
            for i in range(KEPT):
                at = c * CHUNK + b * KEPT + i
                y = over_modes(out_pow[i] * state)
                for j in range(i + 1):
                    y = y + response[j] * u_ref[at - j]
                y_ref[at] = y
        return carry

    lax.fori_loop(0, chunks, y_chunk, 0)

    device_decay = jnp.exp(lam * (-1.0 * rows))
    lead = jnp.exp(per_mode(lam) * (-1.0 * steps * segment.astype(F32)))
    for copy in states:
        copy.wait()
    incoming = jnp.zeros((modes, width), F32)
    for k in range(n_ctx - 1, 0, -1):
        reached = (ctx >= k).astype(F32)
        incoming = device_decay * incoming + got_state[k].astype(F32) * reached

    lane = lax.broadcasted_iota(jnp.int32, (SEG, LANES), 1)
    half = chunks // 2
    gain = in_all(gain_ref[...])

    def mix_chunk(c, carry):
        far, power = carry
        place = lane - (c % half) * CHUNK
        for t in range(CHUNK):
            at = c * CHUNK + t
            far = decay_b * far
            mixed = qs_ref[at] * (y_ref[at] + over_modes(far))
            mix_ref[pl.ds(at, SEG, stride=steps), :] = mixed * gain
            power = jnp.where(
                place == t, jnp.sum(mixed * mixed, axis=1, keepdims=True), power
            )
        return far, power

    far = coef_b * (start + lead * per_mode(incoming))
    no_power = jnp.zeros((SEG, LANES), F32)
    far, power = mix_chunk(0, (far, no_power))
    far, power_0 = lax.fori_loop(1, half, mix_chunk, (far + coef_b * first, power))
    _, power_1 = lax.fori_loop(half, chunks, mix_chunk, (far, no_power))

    own = jnp.concatenate([power_0, power_1], axis=0)
    send_x[...] = own
    over_x = [
        pltpu.make_async_remote_copy(
            src_ref=send_x,
            dst_ref=got_x.at[k],
            send_sem=x_s.at[k],
            recv_sem=x_r.at[k],
            device_id=along_x(k),
            device_id_type=MESH,
        )
        for k in range(1, X_CHIPS)
    ]
    for copy in over_x:
        copy.start()
    for copy in over_x:
        copy.wait()
    own = own + sum(got_x[k] for k in range(1, X_CHIPS))
    send_z[...] = own.astype(BF16)
    over_z = [
        pltpu.make_async_remote_copy(
            src_ref=send_z,
            dst_ref=got_z.at[k],
            send_sem=z_s.at[k],
            recv_sem=z_r.at[k],
            device_id=along_z(k),
            device_id_type=MESH,
        )
        for k in range(1, z_chips)
    ]
    for copy in over_z:
        copy.start()
    for copy in over_z:
        copy.wait()
    sum_ref[...] = own + sum(got_z[k].astype(F32) for k in range(1, z_chips))


def finish(channels, mix_ref, sum_ref, out_hbm, out_v, out_sem):
    groups = sum_ref.shape[0]
    scale = lax.rsqrt(sum_ref[...] * (1.0 / channels) + 1e-05)
    padded = jnp.concatenate(
        [scale, jnp.zeros((LANES - groups, LANES), F32)], axis=0
    )
    columns = padded.T
    halves = groups // SEG
    outs = []
    for g in range(groups):
        row = (g % halves) * SEG + g // halves
        spread = jnp.broadcast_to(columns[:, row : row + 1], (LANES, LANES))
        at = pl.ds(g * LANES, LANES)
        out_v[at, :] = (mix_ref[at, :] * spread).astype(BF16)
        if g % 4 == 3:
            span = pl.ds((g - 3) * LANES, 4 * LANES)
            copy = pltpu.make_async_copy(out_v.at[span], out_hbm.at[span], out_sem.at[g // 4])
            copy.start()
            outs.append(copy)
    for copy in outs:
        copy.wait()


def shards(n_ctx, n_chan, queries, keys_in, values_in, short_weights, decay_rates, residues, skip_term, out_gain):
    rows, width = queries.shape[1:]
    taps, modes = short_weights.shape[1], decay_rates.shape[0]
    steps, groups = rows // SEG, rows // LANES
    z_chips = n_chan // X_CHIPS
    dma = pltpu.SemaphoreType.DMA
    vmem = pl.BlockSpec(memory_space=pltpu.VMEM)
    hbm = pl.BlockSpec(memory_space=pltpu.HBM)
    mixed, sums = pl.pallas_call(
        functools.partial(body, (n_ctx, n_chan, width, taps, modes)),
        out_shape=(
            jax.ShapeDtypeStruct((rows, width), F32),
            jax.ShapeDtypeStruct((groups, LANES), F32),
        ),
        in_specs=[hbm] * 8,
        out_specs=(vmem, vmem),
        scratch_shapes=[
            pltpu.VMEM((3, rows, width), BF16),
            pltpu.VMEM((3, taps, width), F32),
            pltpu.VMEM((modes, width), F32),
            pltpu.VMEM((modes, width), F32),
            pltpu.VMEM((1, width), F32),
            pltpu.VMEM((1, width), F32),
            pltpu.VMEM((3, HALO, width), BF16),
            pltpu.VMEM((steps, SEG, width), F32),
            pltpu.VMEM((steps, SEG, width), F32),
            pltpu.VMEM((steps, SEG, width), F32),
            pltpu.VMEM((steps // KEPT, modes, SEG, width), F32),
            pltpu.VMEM((KEPT, modes, SEG, width), F32),
            pltpu.VMEM((modes, width), BF16),
            pltpu.VMEM((n_ctx, modes, width), BF16),
            pltpu.VMEM((groups, LANES), F32),
            pltpu.VMEM((X_CHIPS, groups, LANES), F32),
            pltpu.VMEM((groups, LANES), BF16),
            pltpu.VMEM((z_chips, groups, LANES), BF16),
            dma((3,)),
            dma((5,)),
            dma((3,)),
            dma((3,)),
            dma((n_ctx,)),
            dma((n_ctx,)),
            dma((X_CHIPS,)),
            dma((X_CHIPS,)),
            dma((z_chips,)),
            dma((z_chips,)),
        ],
        compiler_params=pltpu.CompilerParams(
            collective_id=0, has_side_effects=True, vmem_limit_bytes=24 << 20
        ),
        name="hyena",
    )(
        *(
            pltpu.with_memory_space_constraint(x, pltpu.HBM)
            for x in (
                queries[0],
                keys_in[0],
                values_in[0],
                short_weights,
                decay_rates,
                residues,
                skip_term[None],
                out_gain[None],
            )
        )
    )
    out = pl.pallas_call(
        functools.partial(finish, width * n_chan),
        out_shape=jax.ShapeDtypeStruct((rows, width), BF16),
        in_specs=[vmem, vmem],
        out_specs=hbm,
        scratch_shapes=[pltpu.VMEM((rows, width), BF16), dma((groups // 4,))],
        compiler_params=pltpu.CompilerParams(vmem_limit_bytes=8 << 20),
        name="finish",
    )(mixed, sums)
    return out[None]


def solution(mesh):
    placed = (
        P(None, "ctx", "chan"),
        P(None, "ctx", "chan"),
        P(None, "ctx", "chan"),
        P(None, None, "chan"),
        P(None, "chan"),
        P(None, "chan"),
        P("chan"),
        P("chan"),
    )
    return jax.shard_map(
        functools.partial(shards, mesh.shape["ctx"], mesh.shape["chan"]),
        mesh=mesh,
        in_specs=placed,
        out_specs=P(None, "ctx", "chan"),
        check_vma=False,
    )
```

time: 44.1 us -> 40.4 us (0.916)
  local copies, waits for them, and re-layouts: 1.87 us -> 0 us
  Pallas kernels: 42.1 us -> 40.3 us
    pallas_call x1, Pallas kernels: 42.1 us -> 39.1 us  [shards(): pl.pallas_call(functools.partial(body, (n_ctx, n_chan, width, taps, modes...]
    unnamed x1 -> x0, local copies, waits for them, and re-layouts: 1.87 us -> none
    pallas_call x0 -> x1, Pallas kernels: none -> 1.17 us  [shards(): pl.pallas_call(functools.partial(finish, width * n_chan), out_shape=jax.S...]
where the time goes in v1:
time: 40.4 us; the launch traced here: 40.3 us
  Pallas kernels  40.3 us (100%)
    pallas_call x1, Pallas kernels, shards(): pl.pallas_call(functools.partial(body, (n_ctx, n_chan, width, taps, modes...  39.1 us
    pallas_call x1, Pallas kernels, shards(): pl.pallas_call(functools.partial(finish, width * n_chan), out_shape=jax.S...  1.17 us

profile of v1, /device:TPU:8, one launch (start us, length us, event | category | flops | bytes accessed | tf_op | source)
XLA Modules:
  0.0 40.3 jit_solution(16140521648503130255)
XLA Ops:
  0.0 39.1 %hyena.1 = (f32[2048,128]{1,0:T(8,128)S(1)}, f32[16,128]{1,0:T(8,128)S(1)}) custom-call(bf16[2048,128]{1,0:T(8,128)(2,1)} %bitcast.6, bf16[2048,128]{1,0:T(8,128)(2,1)} %bitcast.7, bf16[2048,128]{1,0:T(8,128)(2,1)} %bitcast.8, f32[3,7,128]{2,1,0:T(8,128)} %w_hbm.1, f32[16,128]{1,0:T(8,128)} %lam_hbm.1, f32[16,128]{1,0:T(8,128)} %res_hbm.1, ...), custom_call_target="tpu_custom_call" | custom-call | tf_op jit(solution)/shard_map/hyena/pallas_call | solution.py:369
  39.1 1.2 %finish.1 = bf16[2048,128]{1,0:T(8,128)(2,1)} custom-call(f32[2048,128]{1,0:T(8,128)S(1)} %get-tuple-element.7.mix_ref, f32[16,128]{1,0:T(8,128)S(1)} %get-tuple-element.8.sum_ref), custom_call_target="tpu_custom_call" | custom-call | tf_op jit(solution)/shard_map/finish/pallas_call | solution.py:426

commit v2 on v1

--- a/solution.py
+++ b/solution.py
@@ -62,8 +62,10 @@
     u_ref,
     qs_ref,
     y_ref,
+    mix_s,
     kept,
     out_pow,
+    scan_w,
     send_state,
     got_state,
     send_x,
@@ -80,6 +82,7 @@
     x_r,
     z_s,
     z_r,
+    near_sem,
 ):
     n_ctx, n_chan, width, taps, modes = sizes
     rows = q_hbm.shape[0]
@@ -89,24 +92,30 @@
     z_chips = n_chan // X_CHIPS
     ctx = lax.axis_index("ctx")
     chan = lax.axis_index("chan")
-    my_x, my_z = chan // z_chips, chan % z_chips
+    my_x, my_z = lax.div(chan, z_chips), lax.rem(chan, z_chips)
+    y_chips = n_ctx // 2
+    my_y, my_core = lax.div(ctx, 2), lax.rem(ctx, 2)
 
     def along_ctx(k):
-        return ((ctx + k) % n_ctx, chan)
+        return (lax.rem(ctx + k, n_ctx), chan)
+
+    def along_y(k, core):
+        return (2 * lax.rem(my_y + (k + y_chips), y_chips) + core, chan)
 
     def along_x(k):
-        return (ctx, ((my_x + k) % X_CHIPS) * z_chips + my_z)
+        return (ctx, lax.rem(my_x + (k + X_CHIPS), X_CHIPS) * z_chips + my_z)
 
     def along_z(k):
-        return (ctx, my_x * z_chips + (my_z + k) % z_chips)
-
-    barrier = pltpu.get_barrier_semaphore()
-    for k in range(1, n_ctx):
-        pl.semaphore_signal(barrier, inc=1, device_id=along_ctx(k), device_id_type=MESH)
-    for k in range(1, X_CHIPS):
-        pl.semaphore_signal(barrier, inc=1, device_id=along_x(k), device_id_type=MESH)
-    for k in range(1, z_chips):
-        pl.semaphore_signal(barrier, inc=1, device_id=along_z(k), device_id_type=MESH)
+        return (ctx, my_x * z_chips + lax.rem(my_z + (k + z_chips), z_chips))
+
+    def all_of(got, *sems):
+        part = got.at[pl.ds(1, got.shape[0] - 1)]
+        for sem in sems:
+            pltpu.make_async_copy(part, part, sem).wait()
+
+    def tell(sem, *others):
+        for other in others:
+            pl.semaphore_signal(sem, inc=1, device_id=other, device_id_type=MESH)
 
     streams = (q_hbm, k_hbm, v_hbm)
     params = [
@@ -127,6 +136,20 @@
     for copy in params:
         copy.start()
     loads[0].start()
+
+    barrier = pltpu.get_barrier_semaphore()
+    tell(
+        barrier,
+        along_y(0, 1 - my_core),
+        along_y(-1, 0),
+        along_y(-1, 1),
+        along_y(1, 0),
+        along_y(1, 1),
+        along_x(-1),
+        along_x(1),
+        along_z(-1),
+        along_z(1),
+    )
     for copy in params:
         copy.wait()
 
@@ -134,7 +157,12 @@
     coef = res_ref[...] * jnp.sqrt(expm1_of_minus(2.0 * lam))
     decay = 1.0 - expm1_of_minus(lam)
     decay_b = per_mode(decay)
-    coef_b = per_mode(coef)
+
+    segment = lax.broadcasted_iota(jnp.int32, (modes, SEG, width), 1)
+    for i in range(3):
+        weight = per_mode(jnp.exp(lam * (-1.0 * steps * 2**i)))
+        scan_w[i] = jnp.where(segment >= 2**i, weight, 0.0)
+    scan_w[3] = per_mode(jnp.exp(lam * (-1.0 * (steps - CHUNK))))
 
     def by_step(i, c):
         parts = [
@@ -166,9 +194,8 @@
     loads[2].wait()
     w_k, w_v = taps_of(1), taps_of(2)
     first_k, first_v = by_step(1, 0)[CHUNK - rim :], by_step(2, 0)[CHUNK - rim :]
-    before = lax.fori_loop(1, chunks // 2, u_chunk, (first_k, first_v))
-
-    pl.semaphore_wait(barrier, (n_ctx - 1) + (X_CHIPS - 1) + (z_chips - 1))
+
+    pl.semaphore_wait(barrier, 9)
     halos = [
         pltpu.make_async_remote_copy(
             src_ref=streams[i].at[pl.ds(rows - HALO, HALO)],
@@ -182,6 +209,15 @@
     ]
     for copy in halos:
         copy.start()
+    tell(near_sem.at[0], along_y(-1, my_core), along_y(1, my_core))
+    tell(near_sem.at[1], along_x(-1), along_x(1))
+    tell(near_sem.at[2], along_z(-1), along_z(1))
+    before = lax.fori_loop(1, chunks // 2, u_chunk, (first_k, first_v))
+
+    for i in range(3):
+        pl.semaphore_wait(near_sem.at[i], 2)
+    tell(near_sem.at[3], along_y(-2, my_core), along_y(2, my_core))
+    tell(near_sem.at[4], along_z(-2), along_z(2))
     tail_k, tail_v = lax.fori_loop(chunks // 2, chunks, u_chunk, before)
 
     def advance(c, state):
@@ -207,15 +243,9 @@
 
     make_u(0, entering(1, tail_k), entering(2, tail_v))
     first = advance(0, zero_state)
-    ends = ends + per_mode(jnp.exp(lam * (-1.0 * (steps - CHUNK)))) * first
-
-    segment = lax.broadcasted_iota(jnp.int32, (modes, SEG, width), 1)
-    total = ends
-    for shift in (1, 2, 4):
-        weight = jnp.where(
-            segment >= shift, per_mode(jnp.exp(lam * (-1.0 * steps * shift))), 0.0
-        )
-        total = total + weight * pltpu.roll(total, shift, 1)
+    total = ends + scan_w[3] * first
+    for i in range(3):
+        total = total + scan_w[i] * pltpu.roll(total, 2**i, 1)
     send_state[...] = total[:, SEG - 1, :].astype(BF16)
     start = jnp.where(segment >= 1, pltpu.roll(total, 1, 1), 0.0)
 
@@ -230,8 +260,11 @@
         )
         for k in range(1, n_ctx)
     ]
+    pl.semaphore_wait(near_sem.at[3], 2)
     for k in sorted(range(1, n_ctx), key=lambda k: abs(k - n_ctx // 2)):
-        states[k - 1].start()
+        pl.when(ctx < n_ctx - k)(states[k - 1].start)
+    pl.semaphore_wait(near_sem.at[4], 2)
+    tell(near_sem.at[5], along_z(-4), along_z(4))
 
     loads[0].wait()
     w_q = taps_of(0)
@@ -268,44 +301,61 @@
 
     device_decay = jnp.exp(lam * (-1.0 * rows))
     lead = jnp.exp(per_mode(lam) * (-1.0 * steps * segment.astype(F32)))
-    for copy in states:
-        copy.wait()
+    for k in range(1, n_ctx):
+        pl.when(ctx < n_ctx - k)(states[k - 1].wait_send)
+        pl.when(ctx >= k)(states[k - 1].wait_recv)
     incoming = jnp.zeros((modes, width), F32)
     for k in range(n_ctx - 1, 0, -1):
-        reached = (ctx >= k).astype(F32)
-        incoming = device_decay * incoming + got_state[k].astype(F32) * reached
+        got = jnp.where(ctx >= k, got_state[k].astype(F32), 0.0)
+        incoming = device_decay * incoming + got
 
     lane = lax.broadcasted_iota(jnp.int32, (SEG, LANES), 1)
+    gain = in_all(gain_ref[...])
+
     half = chunks // 2
-    gain = in_all(gain_ref[...])
-
-    def mix_chunk(c, carry):
-        far, power = carry
-        place = lane - (c % half) * CHUNK
+
+    def with_power_of(c, power, base):
+        place = lane - (c - base) * CHUNK
         for t in range(CHUNK):
-            at = c * CHUNK + t
-            far = decay_b * far
-            mixed = qs_ref[at] * (y_ref[at] + over_modes(far))
-            mix_ref[pl.ds(at, SEG, stride=steps), :] = mixed * gain
+            mixed = mix_s[c * CHUNK + t]
             power = jnp.where(
                 place == t, jnp.sum(mixed * mixed, axis=1, keepdims=True), power
             )
-        return far, power
-
-    far = coef_b * (start + lead * per_mode(incoming))
+        return power
+
+    def mix_chunk(c, far):
+        for t in range(CHUNK):
+            at = c * CHUNK + t
+            y = y_ref[at] + over_modes(out_pow[t % KEPT] * far)
+            mix_s[at] = qs_ref[at] * y
+            if t % KEPT == KEPT - 1:
+                far = decay_kept * far
+        return far
+
+    def mix_and_power(c, carry, base):
+        far, power = carry
+        power = with_power_of(c - 1, power, base)
+        return mix_chunk(c, far), power
+
+    decay_kept = per_mode((decay * decay) * (decay * decay))
     no_power = jnp.zeros((SEG, LANES), F32)
-    far, power = mix_chunk(0, (far, no_power))
-    far, power_0 = lax.fori_loop(1, half, mix_chunk, (far + coef_b * first, power))
-    _, power_1 = lax.fori_loop(half, chunks, mix_chunk, (far, no_power))
+    far = mix_chunk(0, start + lead * per_mode(incoming)) + first
+    far, power_0 = lax.fori_loop(
+        1, half + 1, functools.partial(mix_and_power, base=0), (far, no_power)
+    )
+    _, power_1 = lax.fori_loop(
+        half + 1, chunks, functools.partial(mix_and_power, base=half), (far, no_power)
+    )
+    power_1 = with_power_of(chunks - 1, power_1, half)
 
     own = jnp.concatenate([power_0, power_1], axis=0)
-    send_x[...] = own
+    send_x[...] = own.astype(BF16)
     over_x = [
         pltpu.make_async_remote_copy(
             src_ref=send_x,
             dst_ref=got_x.at[k],
-            send_sem=x_s.at[k],
-            recv_sem=x_r.at[k],
+            send_sem=x_s,
+            recv_sem=x_r,
             device_id=along_x(k),
             device_id_type=MESH,
         )
@@ -313,40 +363,45 @@
     ]
     for copy in over_x:
         copy.start()
-    for copy in over_x:
-        copy.wait()
-    own = own + sum(got_x[k] for k in range(1, X_CHIPS))
+
+    def relayout(c, carry):
+        at = pl.ds(pl.multiple_of(c * CHUNK, CHUNK), CHUNK)
+        by_segment = jnp.swapaxes(mix_s[at] * gain, 0, 1)
+        for s in range(SEG):
+            to = pl.multiple_of(s * steps + c * CHUNK, CHUNK)
+            mix_ref[pl.ds(to, CHUNK), :] = by_segment[s]
+        return carry
+
+    lax.fori_loop(0, chunks, relayout, 0)
+    all_of(got_x, x_s, x_r)
+    own = own + sum(got_x[k].astype(F32) for k in range(1, X_CHIPS))
     send_z[...] = own.astype(BF16)
     over_z = [
         pltpu.make_async_remote_copy(
             src_ref=send_z,
             dst_ref=got_z.at[k],
-            send_sem=z_s.at[k],
-            recv_sem=z_r.at[k],
+            send_sem=z_s,
+            recv_sem=z_r,
             device_id=along_z(k),
             device_id_type=MESH,
         )
         for k in range(1, z_chips)
     ]
+    pl.semaphore_wait(near_sem.at[5], 2)
     for copy in over_z:
         copy.start()
-    for copy in over_z:
-        copy.wait()
+    all_of(got_z, z_s, z_r)
     sum_ref[...] = own + sum(got_z[k].astype(F32) for k in range(1, z_chips))
 
 
 def finish(channels, mix_ref, sum_ref, out_hbm, out_v, out_sem):
     groups = sum_ref.shape[0]
     scale = lax.rsqrt(sum_ref[...] * (1.0 / channels) + 1e-05)
-    padded = jnp.concatenate(
-        [scale, jnp.zeros((LANES - groups, LANES), F32)], axis=0
-    )
-    columns = padded.T
     halves = groups // SEG
     outs = []
     for g in range(groups):
         row = (g % halves) * SEG + g // halves
-        spread = jnp.broadcast_to(columns[:, row : row + 1], (LANES, LANES))
+        spread = jnp.broadcast_to(scale[row : row + 1], (LANES, LANES)).T
         at = pl.ds(g * LANES, LANES)
         out_v[at, :] = (mix_ref[at, :] * spread).astype(BF16)
         if g % 4 == 3:
@@ -385,12 +440,14 @@
             pltpu.VMEM((steps, SEG, width), F32),
             pltpu.VMEM((steps, SEG, width), F32),
             pltpu.VMEM((steps, SEG, width), F32),
+            pltpu.VMEM((steps, SEG, width), F32),
             pltpu.VMEM((steps // KEPT, modes, SEG, width), F32),
             pltpu.VMEM((KEPT, modes, SEG, width), F32),
+            pltpu.VMEM((4, modes, SEG, width), F32),
             pltpu.VMEM((modes, width), BF16),
             pltpu.VMEM((n_ctx, modes, width), BF16),
-            pltpu.VMEM((groups, LANES), F32),
-            pltpu.VMEM((X_CHIPS, groups, LANES), F32),
+            pltpu.VMEM((groups, LANES), BF16),
+            pltpu.VMEM((X_CHIPS, groups, LANES), BF16),
             pltpu.VMEM((groups, LANES), BF16),
             pltpu.VMEM((z_chips, groups, LANES), BF16),
             dma((3,)),
@@ -399,10 +456,11 @@
             dma((3,)),
             dma((n_ctx,)),
             dma((n_ctx,)),
-            dma((X_CHIPS,)),
-            dma((X_CHIPS,)),
-            dma((z_chips,)),
-            dma((z_chips,)),
+            dma,
+            dma,
+            dma,
+            dma,
+            pltpu.SemaphoreType.REGULAR((6,)),
         ],
         compiler_params=pltpu.CompilerParams(
             collective_id=0, has_side_effects=True, vmem_limit_bytes=24 << 20

time: 40.4 us -> 36.8 us (0.911)
  the two profiles are of different devices: /device:TPU:8 before, /device:TPU:56 now
where the time goes in v2:
time: 36.8 us; the launch traced here: 36.6 us
  Pallas kernels  36.6 us (99%)
    pallas_call x1, Pallas kernels, shards(): pl.pallas_call(functools.partial(body, (n_ctx, n_chan, width, taps, modes...  35.6 us
    pallas_call x1, Pallas kernels, shards(): pl.pallas_call(functools.partial(finish, width * n_chan), out_shape=jax.S...  1.04 us

profile of v2, /device:TPU:56, one launch (start us, length us, event | category | flops | bytes accessed | tf_op | source)
XLA Modules:
  0.0 36.6 jit_solution(13146773656641887039)
XLA Ops:
  0.0 35.6 %hyena.1 = (f32[2048,128]{1,0:T(8,128)S(1)}, f32[16,128]{1,0:T(8,128)S(1)}) custom-call(bf16[2048,128]{1,0:T(8,128)(2,1)} %bitcast.6, bf16[2048,128]{1,0:T(8,128)(2,1)} %bitcast.7, bf16[2048,128]{1,0:T(8,128)(2,1)} %bitcast.8, f32[3,7,128]{2,1,0:T(8,128)} %w_hbm.1, f32[16,128]{1,0:T(8,128)} %lam_hbm.1, f32[16,128]{1,0:T(8,128)} %res_hbm.1, ...), custom_call_target="tpu_custom_call" | custom-call | tf_op jit(solution)/shard_map/hyena/pallas_call | solution.py:424
  35.6 1.0 %finish.1 = bf16[2048,128]{1,0:T(8,128)(2,1)} custom-call(f32[2048,128]{1,0:T(8,128)S(1)} %get-tuple-element.7.mix_ref, f32[16,128]{1,0:T(8,128)S(1)} %get-tuple-element.8.sum_ref), custom_call_target="tpu_custom_call" | custom-call | tf_op jit(solution)/shard_map/finish/pallas_call | solution.py:484

commit v3 on v2

--- a/solution.py
+++ b/solution.py
@@ -280,8 +280,9 @@
 
     response = []
     power_of = coef
-    for i in range(KEPT):
-        response.append(in_all(jnp.sum(power_of, axis=0, keepdims=True)))
+    for i in range(CHUNK):
+        if i < KEPT:
+            response.append(in_all(jnp.sum(power_of, axis=0, keepdims=True)))
         power_of = power_of * decay
         out_pow[i] = per_mode(power_of)
     response[0] = response[0] + in_all(skip_ref[...])
@@ -299,15 +300,21 @@
 
     lax.fori_loop(0, chunks, y_chunk, 0)
 
-    device_decay = jnp.exp(lam * (-1.0 * rows))
     lead = jnp.exp(per_mode(lam) * (-1.0 * steps * segment.astype(F32)))
+    decay_chunk = per_mode(jnp.exp(lam * (-1.0 * CHUNK)))
+    reach = [
+        jnp.where(ctx >= k, jnp.exp(lam * (-1.0 * rows * (k - 1))), 0.0)
+        for k in range(1, n_ctx)
+    ]
     for k in range(1, n_ctx):
-        pl.when(ctx < n_ctx - k)(states[k - 1].wait_send)
         pl.when(ctx >= k)(states[k - 1].wait_recv)
-    incoming = jnp.zeros((modes, width), F32)
-    for k in range(n_ctx - 1, 0, -1):
-        got = jnp.where(ctx >= k, got_state[k].astype(F32), 0.0)
-        incoming = device_decay * incoming + got
+    terms = [
+        jnp.where(ctx >= k, got_state[k].astype(F32), 0.0) * reach[k - 1]
+        for k in range(1, n_ctx)
+    ]
+    while len(terms) > 1:
+        terms = [sum(terms[i : i + 2]) for i in range(0, len(terms), 2)]
+    incoming = terms[0]
 
     lane = lax.broadcasted_iota(jnp.int32, (SEG, LANES), 1)
     gain = in_all(gain_ref[...])
@@ -317,7 +324,7 @@
     def with_power_of(c, power, base):
         place = lane - (c - base) * CHUNK
         for t in range(CHUNK):
-            mixed = mix_s[c * CHUNK + t]
+            mixed = mix_s[(c + 1) * CHUNK + t]
             power = jnp.where(
                 place == t, jnp.sum(mixed * mixed, axis=1, keepdims=True), power
             )
@@ -326,25 +333,26 @@
     def mix_chunk(c, far):
         for t in range(CHUNK):
             at = c * CHUNK + t
-            y = y_ref[at] + over_modes(out_pow[t % KEPT] * far)
-            mix_s[at] = qs_ref[at] * y
-            if t % KEPT == KEPT - 1:
-                far = decay_kept * far
-        return far
-
-    def mix_and_power(c, carry, base):
+            y = y_ref[at] + over_modes(out_pow[t] * far)
+            mix_s[at + CHUNK] = qs_ref[at] * y
+        return decay_chunk * far
+
+    def mix_pair(p, carry, base):
         far, power = carry
-        power = with_power_of(c - 1, power, base)
-        return mix_chunk(c, far), power
-
-    decay_kept = per_mode((decay * decay) * (decay * decay))
+        power = with_power_of(2 * p - 1, power, base)
+        far = mix_chunk(2 * p, far) + first * (p == 0).astype(F32)
+        power = with_power_of(2 * p, power, base)
+        return mix_chunk(2 * p + 1, far), power
+
     no_power = jnp.zeros((SEG, LANES), F32)
-    far = mix_chunk(0, start + lead * per_mode(incoming)) + first
+    mix_s[0:CHUNK] = jnp.zeros((CHUNK, SEG, width), F32)
+    far = start + lead * per_mode(incoming)
     far, power_0 = lax.fori_loop(
-        1, half + 1, functools.partial(mix_and_power, base=0), (far, no_power)
+        0, half // 2, functools.partial(mix_pair, base=0), (far, no_power)
     )
+    power_0 = with_power_of(half - 1, power_0, 0)
     _, power_1 = lax.fori_loop(
-        half + 1, chunks, functools.partial(mix_and_power, base=half), (far, no_power)
+        half // 2, half, functools.partial(mix_pair, base=half), (far, no_power)
     )
     power_1 = with_power_of(chunks - 1, power_1, half)
 
@@ -365,7 +373,7 @@
         copy.start()
 
     def relayout(c, carry):
-        at = pl.ds(pl.multiple_of(c * CHUNK, CHUNK), CHUNK)
+        at = pl.ds(pl.multiple_of((c + 1) * CHUNK, CHUNK), CHUNK)
         by_segment = jnp.swapaxes(mix_s[at] * gain, 0, 1)
         for s in range(SEG):
             to = pl.multiple_of(s * steps + c * CHUNK, CHUNK)
@@ -373,7 +381,9 @@
         return carry
 
     lax.fori_loop(0, chunks, relayout, 0)
-    all_of(got_x, x_s, x_r)
+    for k in range(1, n_ctx):
+        pl.when(ctx < n_ctx - k)(states[k - 1].wait_send)
+    all_of(got_x, x_r)
     own = own + sum(got_x[k].astype(F32) for k in range(1, X_CHIPS))
     send_z[...] = own.astype(BF16)
     over_z = [
@@ -390,18 +400,35 @@
     pl.semaphore_wait(near_sem.at[5], 2)
     for copy in over_z:
         copy.start()
-    all_of(got_z, z_s, z_r)
-    sum_ref[...] = own + sum(got_z[k].astype(F32) for k in range(1, z_chips))
+    all_of(got_x, x_s)
+    all_of(got_z, z_s)
+    all_of(got_z, z_r)
+    terms = [own] + [got_z[k].astype(F32) for k in range(1, z_chips)]
+    while len(terms) > 1:
+        terms = [sum(terms[i : i + 2]) for i in range(0, len(terms), 2)]
+    sum_ref[...] = terms[0]
 
 
 def finish(channels, mix_ref, sum_ref, out_hbm, out_v, out_sem):
     groups = sum_ref.shape[0]
     scale = lax.rsqrt(sum_ref[...] * (1.0 / channels) + 1e-05)
+    high = scale.astype(BF16).astype(F32)
+    middle = (scale - high).astype(BF16).astype(F32)
+    low = scale - high - middle
+    unused = jnp.zeros((LANES - 3 * groups, LANES), F32)
+    columns = jnp.concatenate([high, middle, low, unused], axis=0).T.astype(BF16)
+    lane = lax.broadcasted_iota(jnp.int32, (LANES, LANES), 1)
+    group_of = jnp.where(lane < 3 * groups, lane % groups, groups)
+    ones = jnp.ones((LANES, LANES), BF16)
     halves = groups // SEG
     outs = []
     for g in range(groups):
         row = (g % halves) * SEG + g // halves
-        spread = jnp.broadcast_to(scale[row : row + 1], (LANES, LANES)).T
+        if g % 2 == 0:
+            picked = jnp.where(group_of == row, columns, jnp.zeros_like(columns))
+            spread = jnp.dot(picked, ones, preferred_element_type=F32)
+        else:
+            spread = jnp.broadcast_to(scale[row : row + 1], (LANES, LANES)).T
         at = pl.ds(g * LANES, LANES)
         out_v[at, :] = (mix_ref[at, :] * spread).astype(BF16)
         if g % 4 == 3:
@@ -440,9 +467,9 @@
             pltpu.VMEM((steps, SEG, width), F32),
             pltpu.VMEM((steps, SEG, width), F32),
             pltpu.VMEM((steps, SEG, width), F32),
-            pltpu.VMEM((steps, SEG, width), F32),
+            pltpu.VMEM((steps + CHUNK, SEG, width), F32),
             pltpu.VMEM((steps // KEPT, modes, SEG, width), F32),
-            pltpu.VMEM((KEPT, modes, SEG, width), F32),
+            pltpu.VMEM((CHUNK, modes, SEG, width), F32),
             pltpu.VMEM((4, modes, SEG, width), F32),
             pltpu.VMEM((modes, width), BF16),
             pltpu.VMEM((n_ctx, modes, width), BF16),

time: 36.8 us -> 36 us (0.978)
  Pallas kernels: 36.6 us -> 35.9 us
    pallas_call x1, Pallas kernels: 35.6 us -> 34.8 us  [shards(): pl.pallas_call(functools.partial(body, (n_ctx, n_chan, width, taps, modes...]
where the time goes in v3:
time: 36 us; the launch traced here: 35.9 us
  Pallas kernels  35.9 us (100%)
    pallas_call x1, Pallas kernels, shards(): pl.pallas_call(functools.partial(body, (n_ctx, n_chan, width, taps, modes...  34.8 us
    pallas_call x1, Pallas kernels, shards(): pl.pallas_call(functools.partial(finish, width * n_chan), out_shape=jax.S...  1.08 us

profile of v3, /device:TPU:56, one launch (start us, length us, event | category | flops | bytes accessed | tf_op | source)
XLA Modules:
  0.0 35.9 jit_solution(7779798912009779787)
XLA Ops:
  0.0 34.8 %hyena.1 = (f32[2048,128]{1,0:T(8,128)S(1)}, f32[16,128]{1,0:T(8,128)S(1)}) custom-call(bf16[2048,128]{1,0:T(8,128)(2,1)} %bitcast.6, bf16[2048,128]{1,0:T(8,128)(2,1)} %bitcast.7, bf16[2048,128]{1,0:T(8,128)(2,1)} %bitcast.8, f32[3,7,128]{2,1,0:T(8,128)} %w_hbm.1, f32[16,128]{1,0:T(8,128)} %lam_hbm.1, f32[16,128]{1,0:T(8,128)} %res_hbm.1, ...), custom_call_target="tpu_custom_call" | custom-call | tf_op jit(solution)/shard_map/hyena/pallas_call | solution.py:451
  34.8 1.1 %finish.1 = bf16[2048,128]{1,0:T(8,128)(2,1)} custom-call(f32[2048,128]{1,0:T(8,128)S(1)} %get-tuple-element.7.mix_ref, f32[16,128]{1,0:T(8,128)S(1)} %get-tuple-element.8.sum_ref), custom_call_target="tpu_custom_call" | custom-call | tf_op jit(solution)/shard_map/finish/pallas_call | solution.py:511

commit v4 on v3

--- a/solution.py
+++ b/solution.py
@@ -85,8 +85,8 @@
     near_sem,
 ):
     n_ctx, n_chan, width, taps, modes = sizes
-    rows = q_hbm.shape[0]
-    steps = rows // SEG
+    steps = q_hbm.shape[1]
+    rows = SEG * steps
     chunks = steps // CHUNK
     rim = taps - 1
     z_chips = n_chan // X_CHIPS
@@ -130,12 +130,24 @@
             )
         )
     ]
-    loads = [pltpu.make_async_copy(streams[i], raw.at[i], in_sem.at[i]) for i in range(3)]
-    loads[1].start()
-    loads[2].start()
+    loads = [
+        [
+            pltpu.make_async_copy(
+                streams[i].at[:, pl.ds(h * (steps // 2), steps // 2)],
+                raw.at[i, :, pl.ds(h * (steps // 2), steps // 2)],
+                in_sem.at[i, h],
+            )
+            for h in range(2)
+        ]
+        for i in range(3)
+    ]
     for copy in params:
         copy.start()
-    loads[0].start()
+    for h in range(2):
+        loads[1][h].start()
+        loads[2][h].start()
+    for h in range(2):
+        loads[0][h].start()
 
     barrier = pltpu.get_barrier_semaphore()
     tell(
@@ -165,11 +177,8 @@
     scan_w[3] = per_mode(jnp.exp(lam * (-1.0 * (steps - CHUNK))))
 
     def by_step(i, c):
-        parts = [
-            raw[i, pl.ds(pl.multiple_of(s * steps + c * CHUNK, CHUNK), CHUNK), :]
-            for s in range(SEG)
-        ]
-        return jnp.swapaxes(jnp.stack(parts).astype(F32), 0, 1)
+        part = raw[i, :, pl.ds(pl.multiple_of(c * CHUNK, CHUNK), CHUNK), :]
+        return jnp.swapaxes(part.astype(F32), 0, 1)
 
     def taps_of(i):
         return [in_all(w_ref[i, j : j + 1, :]) for j in range(taps)]
@@ -190,15 +199,15 @@
     def u_chunk(c, before):
         return make_u(c, *before)
 
-    loads[1].wait()
-    loads[2].wait()
+    for i in (1, 2):
+        loads[i][0].wait()
     w_k, w_v = taps_of(1), taps_of(2)
     first_k, first_v = by_step(1, 0)[CHUNK - rim :], by_step(2, 0)[CHUNK - rim :]
 
     pl.semaphore_wait(barrier, 9)
     halos = [
         pltpu.make_async_remote_copy(
-            src_ref=streams[i].at[pl.ds(rows - HALO, HALO)],
+            src_ref=streams[i].at[SEG - 1, pl.ds(steps - HALO, HALO)],
             dst_ref=halo.at[i],
             send_sem=halo_s.at[i],
             recv_sem=halo_r.at[i],
@@ -214,11 +223,12 @@
     tell(near_sem.at[2], along_z(-1), along_z(1))
     before = lax.fori_loop(1, chunks // 2, u_chunk, (first_k, first_v))
 
-    for i in range(3):
-        pl.semaphore_wait(near_sem.at[i], 2)
+    for i in (1, 2):
+        loads[i][1].wait()
+    tail_k, tail_v = lax.fori_loop(chunks // 2, chunks, u_chunk, before)
+
+    pl.semaphore_wait(near_sem.at[0], 2)
     tell(near_sem.at[3], along_y(-2, my_core), along_y(2, my_core))
-    tell(near_sem.at[4], along_z(-2), along_z(2))
-    tail_k, tail_v = lax.fori_loop(chunks // 2, chunks, u_chunk, before)
 
     def advance(c, state):
         for t in range(CHUNK):
@@ -231,6 +241,9 @@
     zero_state = jnp.zeros((modes, SEG, width), F32)
     ends = lax.fori_loop(1, chunks, advance, zero_state)
 
+    pl.semaphore_wait(near_sem.at[1], 2)
+    pl.semaphore_wait(near_sem.at[2], 2)
+    tell(near_sem.at[4], along_z(-2), along_z(2))
     for copy in halos:
         copy.wait()
     has_before = (ctx > 0).astype(F32)
@@ -263,10 +276,9 @@
     pl.semaphore_wait(near_sem.at[3], 2)
     for k in sorted(range(1, n_ctx), key=lambda k: abs(k - n_ctx // 2)):
         pl.when(ctx < n_ctx - k)(states[k - 1].start)
-    pl.semaphore_wait(near_sem.at[4], 2)
-    tell(near_sem.at[5], along_z(-4), along_z(4))
-
-    loads[0].wait()
+
+    for copy in loads[0]:
+        copy.wait()
     w_q = taps_of(0)
 
     def q_chunk(c, before_q):
@@ -277,6 +289,9 @@
 
     tail_q = by_step(0, chunks - 1)[CHUNK - rim :]
     lax.fori_loop(0, chunks, q_chunk, entering(0, tail_q))
+
+    pl.semaphore_wait(near_sem.at[4], 2)
+    tell(near_sem.at[5], along_z(-4), along_z(4))
 
     response = []
     power_of = coef
@@ -412,23 +427,11 @@
 def finish(channels, mix_ref, sum_ref, out_hbm, out_v, out_sem):
     groups = sum_ref.shape[0]
     scale = lax.rsqrt(sum_ref[...] * (1.0 / channels) + 1e-05)
-    high = scale.astype(BF16).astype(F32)
-    middle = (scale - high).astype(BF16).astype(F32)
-    low = scale - high - middle
-    unused = jnp.zeros((LANES - 3 * groups, LANES), F32)
-    columns = jnp.concatenate([high, middle, low, unused], axis=0).T.astype(BF16)
-    lane = lax.broadcasted_iota(jnp.int32, (LANES, LANES), 1)
-    group_of = jnp.where(lane < 3 * groups, lane % groups, groups)
-    ones = jnp.ones((LANES, LANES), BF16)
     halves = groups // SEG
     outs = []
     for g in range(groups):
         row = (g % halves) * SEG + g // halves
-        if g % 2 == 0:
-            picked = jnp.where(group_of == row, columns, jnp.zeros_like(columns))
-            spread = jnp.dot(picked, ones, preferred_element_type=F32)
-        else:
-            spread = jnp.broadcast_to(scale[row : row + 1], (LANES, LANES)).T
+        spread = jnp.broadcast_to(scale[row : row + 1], (LANES, LANES)).T
         at = pl.ds(g * LANES, LANES)
         out_v[at, :] = (mix_ref[at, :] * spread).astype(BF16)
         if g % 4 == 3:
@@ -457,7 +460,7 @@
         in_specs=[hbm] * 8,
         out_specs=(vmem, vmem),
         scratch_shapes=[
-            pltpu.VMEM((3, rows, width), BF16),
+            pltpu.VMEM((3, SEG, steps, width), BF16),
             pltpu.VMEM((3, taps, width), F32),
             pltpu.VMEM((modes, width), F32),
             pltpu.VMEM((modes, width), F32),
@@ -477,7 +480,7 @@
             pltpu.VMEM((X_CHIPS, groups, LANES), BF16),
             pltpu.VMEM((groups, LANES), BF16),
             pltpu.VMEM((z_chips, groups, LANES), BF16),
-            dma((3,)),
+            dma((3, 2)),
             dma((5,)),
             dma((3,)),
             dma((3,)),
@@ -497,9 +500,9 @@
         *(
             pltpu.with_memory_space_constraint(x, pltpu.HBM)
             for x in (
-                queries[0],
-                keys_in[0],
-                values_in[0],
+                queries.reshape(SEG, steps, width),
+                keys_in.reshape(SEG, steps, width),
+                values_in.reshape(SEG, steps, width),
                 short_weights,
                 decay_rates,
                 residues,

time: 36 us -> 35.6 us (0.989)
  Pallas kernels: 35.9 us -> 35.4 us
    pallas_call x1, Pallas kernels: 34.8 us -> 34.3 us  [shards(): pl.pallas_call(functools.partial(body, (n_ctx, n_chan, width, taps, modes...]
where the time goes in v4:
time: 35.6 us; the launch traced here: 35.4 us
  Pallas kernels  35.4 us (99%)
    pallas_call x1, Pallas kernels, shards(): pl.pallas_call(functools.partial(body, (n_ctx, n_chan, width, taps, modes...  34.3 us
    pallas_call x1, Pallas kernels, shards(): pl.pallas_call(functools.partial(finish, width * n_chan), out_shape=jax.S...  1.04 us

profile of v4, /device:TPU:56, one launch (start us, length us, event | category | flops | bytes accessed | tf_op | source)
XLA Modules:
  0.0 35.4 jit_solution(8889198919679532283)
XLA Ops:
  0.0 34.3 %hyena.1 = (f32[2048,128]{1,0:T(8,128)S(1)}, f32[16,128]{1,0:T(8,128)S(1)}) custom-call(bf16[8,256,128]{2,1,0:T(8,128)(2,1)} %bitcast.6, bf16[8,256,128]{2,1,0:T(8,128)(2,1)} %bitcast.7, bf16[8,256,128]{2,1,0:T(8,128)(2,1)} %bitcast.8, f32[3,7,128]{2,1,0:T(8,128)} %w_hbm.1, f32[16,128]{1,0:T(8,128)} %lam_hbm.1, f32[16,128]{1,0:T(8,128)} %res_hbm.1, ...), custom_call_target="tpu_custom_call" | custom-call | tf_op jit(solution)/shard_map/hyena/pallas_call | solution.py:454
  34.3 1.0 %finish.1 = bf16[2048,128]{1,0:T(8,128)(2,1)} custom-call(f32[2048,128]{1,0:T(8,128)S(1)} %get-tuple-element.7.mix_ref, f32[16,128]{1,0:T(8,128)S(1)} %get-tuple-element.8.sum_ref), custom_call_target="tpu_custom_call" | custom-call | tf_op jit(solution)/shard_map/finish/pallas_call | solution.py:514

commit v5 on v4

--- a/solution.py
+++ b/solution.py
@@ -150,13 +150,12 @@
         loads[0][h].start()
 
     barrier = pltpu.get_barrier_semaphore()
+    second = my_core == 1
+    pl.when(second)(lambda: tell(barrier, along_y(1, 1)))
     tell(
         barrier,
         along_y(0, 1 - my_core),
-        along_y(-1, 0),
         along_y(-1, 1),
-        along_y(1, 0),
-        along_y(1, 1),
         along_x(-1),
         along_x(1),
         along_z(-1),
@@ -204,7 +203,6 @@
     w_k, w_v = taps_of(1), taps_of(2)
     first_k, first_v = by_step(1, 0)[CHUNK - rim :], by_step(2, 0)[CHUNK - rim :]
 
-    pl.semaphore_wait(barrier, 9)
     halos = [
         pltpu.make_async_remote_copy(
             src_ref=streams[i].at[SEG - 1, pl.ds(steps - HALO, HALO)],
@@ -216,19 +214,35 @@
         )
         for i in range(3)
     ]
-    for copy in halos:
-        copy.start()
-    tell(near_sem.at[0], along_y(-1, my_core), along_y(1, my_core))
-    tell(near_sem.at[1], along_x(-1), along_x(1))
-    tell(near_sem.at[2], along_z(-1), along_z(1))
+
+    def pass_on():
+        for copy in halos:
+            copy.start()
+        tell(near_sem.at[1], along_x(-1), along_x(1))
+        tell(near_sem.at[2], along_z(-1), along_z(1))
+
+    @pl.when(second)
+    def _():
+        pl.semaphore_wait(barrier, 8)
+        tell(near_sem.at[0], along_y(-1, 1), along_y(1, 1))
+        pass_on()
+
     before = lax.fori_loop(1, chunks // 2, u_chunk, (first_k, first_v))
 
     for i in (1, 2):
         loads[i][1].wait()
     tail_k, tail_v = lax.fori_loop(chunks // 2, chunks, u_chunk, before)
 
-    pl.semaphore_wait(near_sem.at[0], 2)
-    tell(near_sem.at[3], along_y(-2, my_core), along_y(2, my_core))
+    @pl.when(second)
+    def _():
+        pl.semaphore_wait(near_sem.at[0], 2)
+        tell(near_sem.at[3], along_y(-2, 1), along_y(2, 1))
+
+    @pl.when(jnp.logical_not(second))
+    def _():
+        pl.semaphore_wait(barrier, 5)
+        pass_on()
+
 
     def advance(c, state):
         for t in range(CHUNK):
@@ -259,23 +273,45 @@
     total = ends + scan_w[3] * first
     for i in range(3):
         total = total + scan_w[i] * pltpu.roll(total, 2**i, 1)
-    send_state[...] = total[:, SEG - 1, :].astype(BF16)
     start = jnp.where(segment >= 1, pltpu.roll(total, 1, 1), 0.0)
-
-    states = [
-        pltpu.make_async_remote_copy(
+    end = total[:, SEG - 1, :]
+    device_decay = jnp.exp(lam * (-1.0 * rows))
+
+    inward = pltpu.make_async_remote_copy(
+        src_ref=send_state,
+        dst_ref=got_state.at[0],
+        send_sem=st_s.at[0],
+        recv_sem=st_r.at[0],
+        device_id=along_ctx(1),
+        device_id_type=MESH,
+    )
+    outward = {
+        (k, core): pltpu.make_async_remote_copy(
             src_ref=send_state,
             dst_ref=got_state.at[k],
-            send_sem=st_s.at[k],
+            send_sem=st_s.at[2 * k + core],
             recv_sem=st_r.at[k],
-            device_id=along_ctx(k),
+            device_id=along_y(k, core),
             device_id_type=MESH,
         )
-        for k in range(1, n_ctx)
-    ]
-    pl.semaphore_wait(near_sem.at[3], 2)
-    for k in sorted(range(1, n_ctx), key=lambda k: abs(k - n_ctx // 2)):
-        pl.when(ctx < n_ctx - k)(states[k - 1].start)
+        for k in range(1, y_chips)
+        for core in range(2)
+    }
+    sends = {key: jnp.logical_and(second, my_y < y_chips - key[0]) for key in outward}
+
+    @pl.when(jnp.logical_not(second))
+    def _():
+        send_state[...] = end.astype(BF16)
+        inward.start()
+
+    @pl.when(second)
+    def _():
+        inward.wait_recv()
+        send_state[...] = (device_decay * got_state[0].astype(F32) + end).astype(BF16)
+        pl.semaphore_wait(near_sem.at[3], 2)
+
+    for key in sorted(outward, key=lambda key: abs(key[0] - y_chips // 2)):
+        pl.when(sends[key])(outward[key].start)
 
     for copy in loads[0]:
         copy.wait()
@@ -318,18 +354,19 @@
     lead = jnp.exp(per_mode(lam) * (-1.0 * steps * segment.astype(F32)))
     decay_chunk = per_mode(jnp.exp(lam * (-1.0 * CHUNK)))
     reach = [
-        jnp.where(ctx >= k, jnp.exp(lam * (-1.0 * rows * (k - 1))), 0.0)
-        for k in range(1, n_ctx)
-    ]
-    for k in range(1, n_ctx):
-        pl.when(ctx >= k)(states[k - 1].wait_recv)
+        jnp.where(my_y >= k, jnp.exp(lam * (-2.0 * rows * (k - 1))), 0.0)
+        for k in range(1, y_chips)
+    ]
+    for k in range(1, y_chips):
+        pl.when(my_y >= k)(outward[k, 0].wait_recv)
     terms = [
-        jnp.where(ctx >= k, got_state[k].astype(F32), 0.0) * reach[k - 1]
-        for k in range(1, n_ctx)
+        jnp.where(my_y >= k, got_state[k].astype(F32), 0.0) * reach[k - 1]
+        for k in range(1, y_chips)
     ]
     while len(terms) > 1:
         terms = [sum(terms[i : i + 2]) for i in range(0, len(terms), 2)]
-    incoming = terms[0]
+    of_core_0 = jnp.where(second, got_state[0].astype(F32), 0.0)
+    incoming = jnp.where(second, device_decay, 1.0) * terms[0] + of_core_0
 
     lane = lax.broadcasted_iota(jnp.int32, (SEG, LANES), 1)
     gain = in_all(gain_ref[...])
@@ -396,8 +433,9 @@
         return carry
 
     lax.fori_loop(0, chunks, relayout, 0)
-    for k in range(1, n_ctx):
-        pl.when(ctx < n_ctx - k)(states[k - 1].wait_send)
+    pl.when(jnp.logical_not(second))(inward.wait_send)
+    for key in outward:
+        pl.when(sends[key])(outward[key].wait_send)
     all_of(got_x, x_r)
     own = own + sum(got_x[k].astype(F32) for k in range(1, X_CHIPS))
     send_z[...] = own.astype(BF16)
@@ -475,7 +513,7 @@
             pltpu.VMEM((CHUNK, modes, SEG, width), F32),
             pltpu.VMEM((4, modes, SEG, width), F32),
             pltpu.VMEM((modes, width), BF16),
-            pltpu.VMEM((n_ctx, modes, width), BF16),
+            pltpu.VMEM((n_ctx // 2, modes, width), BF16),
             pltpu.VMEM((groups, LANES), BF16),
             pltpu.VMEM((X_CHIPS, groups, LANES), BF16),
             pltpu.VMEM((groups, LANES), BF16),
@@ -485,7 +523,7 @@
             dma((3,)),
             dma((3,)),
             dma((n_ctx,)),
-            dma((n_ctx,)),
+            dma((n_ctx // 2,)),
             dma,
             dma,
             dma,

time: 35.6 us -> 34.8 us (0.978)
  Pallas kernels: 35.4 us -> 34.6 us
    pallas_call x1, Pallas kernels: 34.3 us -> 33.5 us  [shards(): pl.pallas_call(functools.partial(body, (n_ctx, n_chan, width, taps, modes...]
where the time goes in v5:
time: 34.8 us; the launch traced here: 34.6 us
  Pallas kernels  34.6 us (99%)
    pallas_call x1, Pallas kernels, shards(): pl.pallas_call(functools.partial(body, (n_ctx, n_chan, width, taps, modes...  33.5 us
    pallas_call x1, Pallas kernels, shards(): pl.pallas_call(functools.partial(finish, width * n_chan), out_shape=jax.S...  1.04 us

profile of v5, /device:TPU:56, one launch (start us, length us, event | category | flops | bytes accessed | tf_op | source)
XLA Modules:
  0.0 34.6 jit_solution(8757571915364252423)
XLA Ops:
  0.0 33.5 %hyena.1 = (f32[2048,128]{1,0:T(8,128)S(1)}, f32[16,128]{1,0:T(8,128)S(1)}) custom-call(bf16[8,256,128]{2,1,0:T(8,128)(2,1)} %bitcast.6, bf16[8,256,128]{2,1,0:T(8,128)(2,1)} %bitcast.7, bf16[8,256,128]{2,1,0:T(8,128)(2,1)} %bitcast.8, f32[3,7,128]{2,1,0:T(8,128)} %w_hbm.1, f32[16,128]{1,0:T(8,128)} %lam_hbm.1, f32[16,128]{1,0:T(8,128)} %res_hbm.1, ...), custom_call_target="tpu_custom_call" | custom-call | tf_op jit(solution)/shard_map/hyena/pallas_call | solution.py:492
  33.5 1.0 %finish.1 = bf16[2048,128]{1,0:T(8,128)(2,1)} custom-call(f32[2048,128]{1,0:T(8,128)S(1)} %get-tuple-element.7.mix_ref, f32[16,128]{1,0:T(8,128)S(1)} %get-tuple-element.8.sum_ref), custom_call_target="tpu_custom_call" | custom-call | tf_op jit(solution)/shard_map/finish/pallas_call | solution.py:552

commit v6 on v5

--- a/solution.py
+++ b/solution.py
@@ -14,6 +14,8 @@
 LANES = 128
 CHUNK = 16
 KEPT = 4
+GROUP = 8
+BY = (7, 8, 5, 4, 4, 4)
 HALO = 16
 X_CHIPS = 4
 
@@ -27,6 +29,15 @@
 
 def per_mode(rows):
     return jnp.broadcast_to(rows[:, None, :], (rows.shape[0], SEG, rows.shape[1]))
+
+
+def loop(first, last, by, step, carry):
+    def some(g, carry):
+        for j in range(by):
+            carry = step(first + g * by + j, carry)
+        return carry
+
+    return lax.fori_loop(0, (last - first) // by, some, carry)
 
 
 def over_modes(terms):
@@ -227,11 +238,11 @@
         tell(near_sem.at[0], along_y(-1, 1), along_y(1, 1))
         pass_on()
 
-    before = lax.fori_loop(1, chunks // 2, u_chunk, (first_k, first_v))
+    before = loop(1, chunks // 2, BY[0], u_chunk, (first_k, first_v))
 
     for i in (1, 2):
         loads[i][1].wait()
-    tail_k, tail_v = lax.fori_loop(chunks // 2, chunks, u_chunk, before)
+    tail_k, tail_v = loop(chunks // 2, chunks, BY[1], u_chunk, before)
 
     @pl.when(second)
     def _():
@@ -253,7 +264,7 @@
         return state
 
     zero_state = jnp.zeros((modes, SEG, width), F32)
-    ends = lax.fori_loop(1, chunks, advance, zero_state)
+    ends = loop(1, chunks, BY[2], advance, zero_state)
 
     pl.semaphore_wait(near_sem.at[1], 2)
     pl.semaphore_wait(near_sem.at[2], 2)
@@ -324,7 +335,7 @@
         return window[CHUNK:]
 
     tail_q = by_step(0, chunks - 1)[CHUNK - rim :]
-    lax.fori_loop(0, chunks, q_chunk, entering(0, tail_q))
+    loop(0, chunks, BY[3], q_chunk, entering(0, tail_q))
 
     pl.semaphore_wait(near_sem.at[4], 2)
     tell(near_sem.at[5], along_z(-4), along_z(4))
@@ -349,7 +360,7 @@
                 y_ref[at] = y
         return carry
 
-    lax.fori_loop(0, chunks, y_chunk, 0)
+    loop(0, chunks, BY[4], y_chunk, 0)
 
     lead = jnp.exp(per_mode(lam) * (-1.0 * steps * segment.astype(F32)))
     decay_chunk = per_mode(jnp.exp(lam * (-1.0 * CHUNK)))
@@ -389,22 +400,24 @@
             mix_s[at + CHUNK] = qs_ref[at] * y
         return decay_chunk * far
 
-    def mix_pair(p, carry, base):
+    def mix_group(p, carry, base):
         far, power = carry
-        power = with_power_of(2 * p - 1, power, base)
-        far = mix_chunk(2 * p, far) + first * (p == 0).astype(F32)
-        power = with_power_of(2 * p, power, base)
-        return mix_chunk(2 * p + 1, far), power
+        for j in range(GROUP):
+            power = with_power_of(GROUP * p + j - 1, power, base)
+            far = mix_chunk(GROUP * p + j, far)
+            if j == 0:
+                far = far + first * (p == 0).astype(F32)
+        return far, power
 
     no_power = jnp.zeros((SEG, LANES), F32)
     mix_s[0:CHUNK] = jnp.zeros((CHUNK, SEG, width), F32)
     far = start + lead * per_mode(incoming)
     far, power_0 = lax.fori_loop(
-        0, half // 2, functools.partial(mix_pair, base=0), (far, no_power)
+        0, half // GROUP, functools.partial(mix_group, base=0), (far, no_power)
     )
     power_0 = with_power_of(half - 1, power_0, 0)
     _, power_1 = lax.fori_loop(
-        half // 2, half, functools.partial(mix_pair, base=half), (far, no_power)
+        half // GROUP, chunks // GROUP, functools.partial(mix_group, base=half), (far, no_power)
     )
     power_1 = with_power_of(chunks - 1, power_1, half)
 
@@ -432,7 +445,7 @@
             mix_ref[pl.ds(to, CHUNK), :] = by_segment[s]
         return carry
 
-    lax.fori_loop(0, chunks, relayout, 0)
+    loop(0, chunks, BY[5], relayout, 0)
     pl.when(jnp.logical_not(second))(inward.wait_send)
     for key in outward:
         pl.when(sends[key])(outward[key].wait_send)

time: 34.8 us -> 33.8 us (0.971)
  Pallas kernels: 34.6 us -> 33.6 us
    pallas_call x1, Pallas kernels: 33.5 us -> 32.6 us  [shards(): pl.pallas_call(functools.partial(body, (n_ctx, n_chan, width, taps, modes...]
where the time goes in v6:
time: 33.8 us; the launch traced here: 33.6 us
  Pallas kernels  33.6 us (99%)
    pallas_call x1, Pallas kernels, shards(): pl.pallas_call(functools.partial(body, (n_ctx, n_chan, width, taps, modes...  32.6 us
    pallas_call x1, Pallas kernels, shards(): pl.pallas_call(functools.partial(finish, width * n_chan), out_shape=jax.S...  1.04 us

profile of v6, /device:TPU:56, one launch (start us, length us, event | category | flops | bytes accessed | tf_op | source)
XLA Modules:
  0.0 33.6 jit_solution(8693296427017703359)
XLA Ops:
  0.0 32.6 %hyena.1 = (f32[2048,128]{1,0:T(8,128)S(1)}, f32[16,128]{1,0:T(8,128)S(1)}) custom-call(bf16[8,256,128]{2,1,0:T(8,128)(2,1)} %bitcast.6, bf16[8,256,128]{2,1,0:T(8,128)(2,1)} %bitcast.7, bf16[8,256,128]{2,1,0:T(8,128)(2,1)} %bitcast.8, f32[3,7,128]{2,1,0:T(8,128)} %w_hbm.1, f32[16,128]{1,0:T(8,128)} %lam_hbm.1, f32[16,128]{1,0:T(8,128)} %res_hbm.1, ...), custom_call_target="tpu_custom_call" | custom-call | tf_op jit(solution)/shard_map/hyena/pallas_call | solution.py:505
  32.6 1.0 %finish.1 = bf16[2048,128]{1,0:T(8,128)(2,1)} custom-call(f32[2048,128]{1,0:T(8,128)S(1)} %get-tuple-element.7.mix_ref, f32[16,128]{1,0:T(8,128)S(1)} %get-tuple-element.8.sum_ref), custom_call_target="tpu_custom_call" | custom-call | tf_op jit(solution)/shard_map/finish/pallas_call | solution.py:565

commit v7 on v6

--- a/solution.py
+++ b/solution.py
@@ -247,7 +247,8 @@
     @pl.when(second)
     def _():
         pl.semaphore_wait(near_sem.at[0], 2)
-        tell(near_sem.at[3], along_y(-2, 1), along_y(2, 1))
+        tell(near_sem.at[3], along_y(-2, 1))
+        tell(near_sem.at[6], along_y(2, 1))
 
     @pl.when(jnp.logical_not(second))
     def _():
@@ -319,10 +320,15 @@
     def _():
         inward.wait_recv()
         send_state[...] = (device_decay * got_state[0].astype(F32) + end).astype(BF16)
-        pl.semaphore_wait(near_sem.at[3], 2)
-
-    for key in sorted(outward, key=lambda key: abs(key[0] - y_chips // 2)):
-        pl.when(sends[key])(outward[key].start)
+
+    reaches_on = my_y < y_chips - 3
+    pl.when(jnp.logical_and(second, reaches_on))(
+        lambda: pl.semaphore_wait(near_sem.at[3], 1)
+    )
+    by_distance = sorted(outward, key=lambda key: -key[0])
+    for key in by_distance:
+        if key[0] <= y_chips // 2:
+            pl.when(sends[key])(outward[key].start)
 
     for copy in loads[0]:
         copy.wait()
@@ -368,6 +374,13 @@
         jnp.where(my_y >= k, jnp.exp(lam * (-2.0 * rows * (k - 1))), 0.0)
         for k in range(1, y_chips)
     ]
+    pl.when(jnp.logical_and(second, jnp.logical_not(reaches_on)))(
+        lambda: pl.semaphore_wait(near_sem.at[3], 1)
+    )
+    pl.when(second)(lambda: pl.semaphore_wait(near_sem.at[6], 1))
+    for key in by_distance[::-1]:
+        if key[0] > y_chips // 2:
+            pl.when(sends[key])(outward[key].start)
     for k in range(1, y_chips):
         pl.when(my_y >= k)(outward[k, 0].wait_recv)
     terms = [
@@ -541,7 +554,7 @@
             dma,
             dma,
             dma,
-            pltpu.SemaphoreType.REGULAR((6,)),
+            pltpu.SemaphoreType.REGULAR((7,)),
         ],
         compiler_params=pltpu.CompilerParams(
             collective_id=0, has_side_effects=True, vmem_limit_bytes=24 << 20

time: 33.8 us -> 36.1 us (1.068)
  Pallas kernels: 33.6 us -> 36 us
    pallas_call x1, Pallas kernels: 32.6 us -> 34.9 us  [shards(): pl.pallas_call(functools.partial(body, (n_ctx, n_chan, width, taps, modes...]
where the time goes in v7:
time: 36.1 us; the launch traced here: 36 us
  Pallas kernels  36 us (100%)
    pallas_call x1, Pallas kernels, shards(): pl.pallas_call(functools.partial(body, (n_ctx, n_chan, width, taps, modes...  34.9 us
    pallas_call x1, Pallas kernels, shards(): pl.pallas_call(functools.partial(finish, width * n_chan), out_shape=jax.S...  1.04 us

profile of v7, /device:TPU:56, one launch (start us, length us, event | category | flops | bytes accessed | tf_op | source)
XLA Modules:
  0.0 36.0 jit_solution(2829705288444721498)
XLA Ops:
  0.0 34.9 %hyena.1 = (f32[2048,128]{1,0:T(8,128)S(1)}, f32[16,128]{1,0:T(8,128)S(1)}) custom-call(bf16[8,256,128]{2,1,0:T(8,128)(2,1)} %bitcast.6, bf16[8,256,128]{2,1,0:T(8,128)(2,1)} %bitcast.7, bf16[8,256,128]{2,1,0:T(8,128)(2,1)} %bitcast.8, f32[3,7,128]{2,1,0:T(8,128)} %w_hbm.1, f32[16,128]{1,0:T(8,128)} %lam_hbm.1, f32[16,128]{1,0:T(8,128)} %res_hbm.1, ...), custom_call_target="tpu_custom_call" | custom-call | tf_op jit(solution)/shard_map/hyena/pallas_call | solution.py:518
  35.0 1.0 %finish.1 = bf16[2048,128]{1,0:T(8,128)(2,1)} custom-call(f32[2048,128]{1,0:T(8,128)S(1)} %get-tuple-element.7.mix_ref, f32[16,128]{1,0:T(8,128)S(1)} %get-tuple-element.8.sum_ref), custom_call_target="tpu_custom_call" | custom-call | tf_op jit(solution)/shard_map/finish/pallas_call | solution.py:578

commit v8 on v6

--- a/solution.py
+++ b/solution.py
@@ -15,7 +15,7 @@
 CHUNK = 16
 KEPT = 4
 GROUP = 8
-BY = (7, 8, 5, 4, 4, 4)
+BY = (7, 8, 15, 4, 8, 4)
 HALO = 16
 X_CHIPS = 4
 
@@ -319,8 +319,11 @@
     def _():
         inward.wait_recv()
         send_state[...] = (device_decay * got_state[0].astype(F32) + end).astype(BF16)
-        pl.semaphore_wait(near_sem.at[3], 2)
-
+
+    reaches_on = my_y < y_chips - 3
+    pl.when(jnp.logical_and(second, reaches_on))(
+        lambda: pl.semaphore_wait(near_sem.at[3], 2)
+    )
     for key in sorted(outward, key=lambda key: abs(key[0] - y_chips // 2)):
         pl.when(sends[key])(outward[key].start)
 
@@ -368,6 +371,9 @@
         jnp.where(my_y >= k, jnp.exp(lam * (-2.0 * rows * (k - 1))), 0.0)
         for k in range(1, y_chips)
     ]
+    pl.when(jnp.logical_and(second, jnp.logical_not(reaches_on)))(
+        lambda: pl.semaphore_wait(near_sem.at[3], 2)
+    )
     for k in range(1, y_chips):
         pl.when(my_y >= k)(outward[k, 0].wait_recv)
     terms = [

time: 33.8 us -> 33.8 us (level)
  no operation moved by 1% of the time
where the time goes in v8:
time: 33.8 us; the launch traced here: 33.6 us
  Pallas kernels  33.6 us (99%)
    pallas_call x1, Pallas kernels, shards(): pl.pallas_call(functools.partial(body, (n_ctx, n_chan, width, taps, modes...  32.6 us
    pallas_call x1, Pallas kernels, shards(): pl.pallas_call(functools.partial(finish, width * n_chan), out_shape=jax.S...  1.04 us

profile of v8, /device:TPU:56, one launch (start us, length us, event | category | flops | bytes accessed | tf_op | source)
XLA Modules:
  0.0 33.6 jit_solution(9141800015341027534)
XLA Ops:
  0.0 32.6 %hyena.1 = (f32[2048,128]{1,0:T(8,128)S(1)}, f32[16,128]{1,0:T(8,128)S(1)}) custom-call(bf16[8,256,128]{2,1,0:T(8,128)(2,1)} %bitcast.6, bf16[8,256,128]{2,1,0:T(8,128)(2,1)} %bitcast.7, bf16[8,256,128]{2,1,0:T(8,128)(2,1)} %bitcast.8, f32[3,7,128]{2,1,0:T(8,128)} %w_hbm.1, f32[16,128]{1,0:T(8,128)} %lam_hbm.1, f32[16,128]{1,0:T(8,128)} %res_hbm.1, ...), custom_call_target="tpu_custom_call" | custom-call | tf_op jit(solution)/shard_map/hyena/pallas_call | solution.py:511
  32.6 1.0 %finish.1 = bf16[2048,128]{1,0:T(8,128)(2,1)} custom-call(f32[2048,128]{1,0:T(8,128)S(1)} %get-tuple-element.7.mix_ref, f32[16,128]{1,0:T(8,128)S(1)} %get-tuple-element.8.sum_ref), custom_call_target="tpu_custom_call" | custom-call | tf_op jit(solution)/shard_map/finish/pallas_call | solution.py:571
